TPU v7x, 32 devices: a whole 2x2x4 slice. The times are simulated.
32 devices in a mesh: dp: 8 (over z, x), tensor: 4 (over y, core).
Axes of the slice: x: 2, y: 2, z: 4, core: 2. Of those that a mesh axis runs over, the one named last changes fastest.
Arguments:
- layer_input: bfloat16 [8192, 512], P(('dp', 'tensor')), may hold values from -6 to 6
- segments: int32 [8, 1024], P('dp'), may hold values from 0 to 3, never falling along the last dimension, each value on 1 to 800 neighbouring positions
- norm1_gain: bfloat16 [512], replicated, may hold values from 0.5 to 1.5
- norm1_bias: bfloat16 [512], replicated, may hold values from -4 to 4
- w_query: bfloat16 [512, 512], P(None, 'tensor'), may hold values from -0.25 to 0.25
- b_query: bfloat16 [512], P('tensor'), may hold values from -6 to 6
- w_key: bfloat16 [512, 512], P(None, 'tensor'), may hold values from -0.25 to 0.25
- w_value: bfloat16 [512, 512], P(None, 'tensor'), may hold values from -0.25 to 0.25
- b_value: bfloat16 [512], P('tensor'), may hold values from -6 to 6
- w_out: bfloat16 [512, 512], P('tensor'), may hold values from -2 to 2
- b_out: bfloat16 [512], replicated, may hold values from -4 to 4
- gate1_w: bfloat16 [512, 512], P('tensor'), may hold values from -0.25 to 0.25
- gate1_b: bfloat16 [512], replicated, may hold values from -6 to 6
- norm2_gain: bfloat16 [512], replicated, may hold values from 0.5 to 1.5
- norm2_bias: bfloat16 [512], replicated, may hold values from -4 to 4
- w_in: bfloat16 [512, 2048], P(None, 'tensor'), may hold values from -0.25 to 0.25
- b_in: bfloat16 [2048], P('tensor'), may hold values from -6 to 6
- w_back: bfloat16 [2048, 512], P('tensor'), may hold values from -0.1875 to 0.1875
- b_back: bfloat16 [512], replicated, may hold values from -4 to 4
- gate2_w: bfloat16 [512, 512], P('tensor'), may hold values from -0.25 to 0.25
- gate2_b: bfloat16 [512], replicated, may hold values from -6 to 6
- cotangent: bfloat16 [8192, 512], P(('dp', 'tensor')), may hold values from -6 to 6
Outputs:
- output: bfloat16 [8192, 512], P(('dp', 'tensor'))
- input_grad: float32 [8192, 512], P(('dp', 'tensor'))
- grad_norm1_gain: float32 [512], replicated
- grad_norm1_bias: float32 [512], replicated
- grad_w_query: float32 [512, 512], P(None, 'tensor')
- grad_b_query: float32 [512], P('tensor')
- grad_w_key: float32 [512, 512], P(None, 'tensor')
- grad_w_value: float32 [512, 512], P(None, 'tensor')
- grad_b_value: float32 [512], P('tensor')
- grad_w_out: float32 [512, 512], P('tensor')
- grad_b_out: float32 [512], replicated
- grad_gate1_w: float32 [512, 512], P('tensor')
- grad_gate1_b: float32 [512], replicated
- grad_norm2_gain: float32 [512], replicated
- grad_norm2_bias: float32 [512], replicated
- grad_w_in: float32 [512, 2048], P(None, 'tensor')
- grad_b_in: float32 [2048], P('tensor')
- grad_w_back: float32 [2048, 512], P('tensor')
- grad_b_back: float32 [512], replicated
- grad_gate2_w: float32 [512, 512], P('tensor')
- grad_gate2_b: float32 [512], replicated
Inputs may be any that keep to these rules, and one draw needn't show every extreme that they name: `segments`: document numbers never fall along a sequence; every sequence holds 4 documents, none longer than 800 tokens, and one document reaches that length.
All inputs are finite; a program needn't handle non-finite values.
Results may differ from a plain program's by a relative error of at most 0.014.
Values may be sent and summed in bfloat16 or wider, within the bound.
No kernel may reach another device: no remote copies, remote signals or barrier semaphores. Data moves between devices by JAX's collectives and lax.ppermute only.
A program may use at most 64 MiB of HBM per device.

v0:
```python
import jax
import jax.numpy as jnp
from jax import lax
from jax.sharding import PartitionSpec as P

HD = 64
EPSILON = 1e-05


def matmul(left, right):
    return jnp.dot(left, right, preferred_element_type=jnp.float32)


def inner_left(left, right):
    return lax.dot_general(
        left, right, (((0,), (0,)), ((), ())), preferred_element_type=jnp.float32
    )


def outer_right(left, right):
    return lax.dot_general(
        left, right, (((1,), (1,)), ((), ())), preferred_element_type=jnp.float32
    )


def column_sum(matrix):
    return jnp.sum(matrix, axis=0, dtype=jnp.float32)


def place_columns(full, piece, start):
    current = lax.dynamic_slice_in_dim(full, start, piece.shape[1], 1)
    return lax.dynamic_update_slice_in_dim(full, current + piece, start, 1)


def smooth_unit(values):
    return jax.nn.gelu(values, approximate=True)


def norm_forward(values, gain, shift):
    centred = values - jnp.mean(values, axis=-1, keepdims=True)
    spread = jnp.mean(centred * centred, axis=-1, keepdims=True)
    inverse = lax.rsqrt(spread + EPSILON)
    unit = centred * inverse
    return (unit * gain + shift, unit, inverse)


def norm_backward(share_grad, unit, inverse, gain):
    scaled = share_grad * gain
    grad_gain = jnp.sum(share_grad * unit, axis=0)
    grad_shift = jnp.sum(share_grad, axis=0)
    average = jnp.mean(scaled, axis=-1, keepdims=True)
    project = jnp.mean(scaled * unit, axis=-1, keepdims=True)
    return (inverse * (scaled - average - unit * project), grad_gain, grad_shift)


def head_major(matrix):
    return matrix.reshape(matrix.shape[0], -1, HD).transpose(1, 0, 2)


def row_major(heads_array):
    return heads_array.transpose(1, 0, 2).reshape(heads_array.shape[1], -1)


def split_blocks(heads_array, count, block):
    return heads_array.reshape(heads_array.shape[0], count, block, HD).transpose(1, 0, 2, 3)


def join_blocks(blocks):
    count, heads, block, width = blocks.shape
    return blocks.transpose(0, 2, 1, 3).reshape(count * block, heads * width)


def build_mask(segment_row):
    places = lax.iota(jnp.int32, segment_row.shape[0])
    same_doc = segment_row[:, None] == segment_row[None, :]
    return same_doc & (places[None, :] <= places[:, None])


def attention_forward(query, keys, values, allowed):
    rows = query.shape[0]
    block = min(512, rows)
    count = rows // block
    scale_factor = HD ** (-0.5)
    heads_k = head_major(keys)
    heads_v = head_major(values)
    query_blocks = split_blocks(head_major(query), count, block)
    mask_blocks = allowed.reshape(count, block, rows)

    def one_block(pieces):
        query_block, mask_block = pieces
        scores = (
            jnp.einsum("hqd,hkd->hqk", query_block, heads_k, preferred_element_type=jnp.float32)
            * scale_factor
        )
        scores = jnp.where(mask_block[None], scores, -1e30)
        totals = jax.nn.logsumexp(scores, axis=-1, keepdims=True)
        probs = jnp.exp(scores - totals).astype(jnp.bfloat16)
        mixed = jnp.einsum("hqk,hkd->hqd", probs, heads_v, preferred_element_type=jnp.float32)
        return (mixed, totals)

    mixed, totals = lax.map(one_block, (query_blocks, mask_blocks))
    return (join_blocks(mixed).astype(jnp.bfloat16), totals)


def attention_backward(query, keys, values, allowed, totals, attended_grad):
    rows = query.shape[0]
    block = min(512, rows)
    count = rows // block
    scale_factor = HD ** (-0.5)
    heads_k = head_major(keys)
    heads_v = head_major(values)
    query_blocks = split_blocks(head_major(query), count, block)
    grad_blocks = split_blocks(head_major(attended_grad), count, block)
    mask_blocks = allowed.reshape(count, block, rows)

    def one_block(carry, pieces):
        key_acc, value_acc = carry
        query_block, grad_block, mask_block, total_block = pieces
        scores = (
            jnp.einsum("hqd,hkd->hqk", query_block, heads_k, preferred_element_type=jnp.float32)
            * scale_factor
        )
        scores = jnp.where(mask_block[None], scores, -1e30)
        probs = jnp.exp(scores - total_block)
        prob_low = probs.astype(jnp.bfloat16)
        prob_grad = jnp.einsum(
            "hqd,hkd->hqk", grad_block, heads_v, preferred_element_type=jnp.float32
        )
        weighted = jnp.sum(probs * prob_grad, axis=-1, keepdims=True)
        score_grad = (probs * (prob_grad - weighted)).astype(jnp.bfloat16)
        query_part = (
            jnp.einsum("hqk,hkd->hqd", score_grad, heads_k, preferred_element_type=jnp.float32)
            * scale_factor
        )
        key_acc = (
            key_acc
            + jnp.einsum(
                "hqk,hqd->hkd", score_grad, query_block, preferred_element_type=jnp.float32
            )
            * scale_factor
        )
        value_acc = value_acc + jnp.einsum(
            "hqk,hqd->hkd", prob_low, grad_block, preferred_element_type=jnp.float32
        )
        return ((key_acc, value_acc), query_part.astype(jnp.bfloat16))

    empty = jnp.zeros(heads_k.shape, jnp.float32)
    (key_acc, value_acc), query_parts = lax.scan(
        one_block, (empty, empty), (query_blocks, grad_blocks, mask_blocks, totals)
    )
    return (
        join_blocks(query_parts),
        row_major(key_acc).astype(jnp.bfloat16),
        row_major(value_acc).astype(jnp.bfloat16),
    )


def forward_pass(layer_input, segments, weights):
    (
        norm1_gain,
        norm1_bias,
        w_query,
        b_query,
        w_key,
        w_value,
        b_value,
        w_out,
        b_out,
        gate1_w,
        gate1_b,
        norm2_gain,
        norm2_bias,
        w_in,
        b_in,
        w_back,
        b_back,
        gate2_w,
        gate2_b,
    ) = weights
    start_col = lax.axis_index("tensor") * gate1_w.shape[0]
    inputs = layer_input.astype(jnp.float32)
    normed_part, unit_one, inverse_one = norm_forward(
        inputs, norm1_gain.astype(jnp.float32), norm1_bias.astype(jnp.float32)
    )
    normed_low = normed_part.astype(jnp.bfloat16)
    normed = lax.all_gather(normed_low, "tensor", axis=0, tiled=True)
    query = (matmul(normed, w_query) + b_query.astype(jnp.float32)).astype(jnp.bfloat16)
    keys = matmul(normed, w_key).astype(jnp.bfloat16)
    values = (matmul(normed, w_value) + b_value.astype(jnp.float32)).astype(jnp.bfloat16)
    allowed = build_mask(segments[0])
    attended, totals = attention_forward(query, keys, values, allowed)
    gate_rows = lax.dynamic_slice_in_dim(normed, start_col, gate1_w.shape[0], 1)
    branch_part, logit_one = (
        lax.psum_scatter(matmul(attended, w_out), "tensor", scatter_dimension=0, tiled=True),
        lax.psum_scatter(matmul(gate_rows, gate1_w), "tensor", scatter_dimension=0, tiled=True),
    )
    branch = branch_part + b_out.astype(jnp.float32)
    gate_one = jax.nn.sigmoid(logit_one + gate1_b.astype(jnp.float32))
    middle = inputs + gate_one * branch
    normed_two_part, unit_two, inverse_two = norm_forward(
        middle, norm2_gain.astype(jnp.float32), norm2_bias.astype(jnp.float32)
    )
    normed_two = lax.all_gather(normed_two_part.astype(jnp.bfloat16), "tensor", axis=0, tiled=True)
    hidden_input = matmul(normed_two, w_in) + b_in.astype(jnp.float32)
    hidden = smooth_unit(hidden_input).astype(jnp.bfloat16)
    gate_rows_two = lax.dynamic_slice_in_dim(normed_two, start_col, gate2_w.shape[0], 1)
    ffn_part, logit_two = (
        lax.psum_scatter(matmul(hidden, w_back), "tensor", scatter_dimension=0, tiled=True),
        lax.psum_scatter(matmul(gate_rows_two, gate2_w), "tensor", scatter_dimension=0, tiled=True),
    )
    ffn_out = ffn_part + b_back.astype(jnp.float32)
    gate_two = jax.nn.sigmoid(logit_two + gate2_b.astype(jnp.float32))
    result = middle + gate_two * ffn_out
    saved = (
        normed,
        normed_low,
        query,
        keys,
        values,
        allowed,
        attended,
        totals,
        branch,
        gate_one,
        unit_one,
        inverse_one,
        normed_two,
        hidden,
        hidden_input,
        ffn_out,
        gate_two,
        unit_two,
        inverse_two,
    )
    return (result, saved)


def body(
    layer_input,
    segments,
    norm1_gain,
    norm1_bias,
    w_query,
    b_query,
    w_key,
    w_value,
    b_value,
    w_out,
    b_out,
    gate1_w,
    gate1_b,
    norm2_gain,
    norm2_bias,
    w_in,
    b_in,
    w_back,
    b_back,
    gate2_w,
    gate2_b,
    cotangent,
):
    weights = (
        norm1_gain,
        norm1_bias,
        w_query,
        b_query,
        w_key,
        w_value,
        b_value,
        w_out,
        b_out,
        gate1_w,
        gate1_b,
        norm2_gain,
        norm2_bias,
        w_in,
        b_in,
        w_back,
        b_back,
        gate2_w,
        gate2_b,
    )
    result, saved = forward_pass(layer_input, segments, weights)
    barrier = lax.optimization_barrier((layer_input, weights))
    unused, saved = forward_pass(barrier[0], segments, barrier[1])
    (
        normed,
        normed_low,
        query,
        keys,
        values,
        allowed,
        attended,
        totals,
        branch,
        gate_one,
        unit_one,
        inverse_one,
        normed_two,
        hidden,
        hidden_input,
        ffn_out,
        gate_two,
        unit_two,
        inverse_two,
    ) = saved
    start_col = lax.axis_index("tensor") * gate1_w.shape[0]
    upstream = cotangent.astype(jnp.float32)
    ffn_grad = (gate_two * upstream).astype(jnp.bfloat16)
    logit_two_grad = (upstream * ffn_out * (gate_two * (1.0 - gate_two))).astype(jnp.bfloat16)
    ffn_grad_all, logit_two_all = (
        lax.all_gather(ffn_grad, "tensor", axis=0, tiled=True),
        lax.all_gather(logit_two_grad, "tensor", axis=0, tiled=True),
    )
    grad_b_back = column_sum(ffn_grad_all)
    grad_gate2_b = column_sum(logit_two_all)
    grad_w_back = inner_left(hidden, ffn_grad_all)
    unused_value, smooth_pull = jax.vjp(smooth_unit, hidden_input)
    hidden_grad = smooth_pull(outer_right(ffn_grad_all, w_back))[0].astype(jnp.bfloat16)
    grad_w_in = inner_left(normed_two, hidden_grad)
    grad_b_in = column_sum(hidden_grad)
    rows_two = lax.dynamic_slice_in_dim(normed_two, start_col, gate2_w.shape[0], 1)
    grad_gate2_w = inner_left(rows_two, logit_two_all)
    normed_two_grad = place_columns(
        outer_right(hidden_grad, w_in), outer_right(logit_two_all, gate2_w), start_col
    )
    normed_two_share = lax.psum_scatter(normed_two_grad, "tensor", scatter_dimension=0, tiled=True)
    middle_back, grad_norm2_gain, grad_norm2_bias = norm_backward(
        normed_two_share, unit_two, inverse_two, norm2_gain.astype(jnp.float32)
    )
    middle_grad = upstream + middle_back
    ffn_grads = (grad_w_in, grad_b_in, grad_w_back, grad_b_back, grad_gate2_w, grad_gate2_b)
    branch_grad = (gate_one * middle_grad).astype(jnp.bfloat16)
    logit_one_grad = (middle_grad * branch * (gate_one * (1.0 - gate_one))).astype(jnp.bfloat16)
    grad_b_out = column_sum(branch_grad)
    grad_gate1_b = column_sum(logit_one_grad)
    branch_all, logit_one_all = (
        lax.all_gather(branch_grad, "tensor", axis=0, tiled=True),
        lax.all_gather(logit_one_grad, "tensor", axis=0, tiled=True),
    )
    grad_w_out = inner_left(attended, branch_all)
    attended_grad = outer_right(branch_all, w_out).astype(jnp.bfloat16)
    rows_one = lax.dynamic_slice_in_dim(normed, start_col, gate1_w.shape[0], 1)
    grad_gate1_w = inner_left(rows_one, logit_one_all)
    query_grad, keys_grad, values_grad = attention_backward(
        query, keys, values, allowed, totals, attended_grad
    )
    grad_w_query = inner_left(normed, query_grad)
    grad_b_query = column_sum(query_grad)
    grad_w_key = inner_left(normed, keys_grad)
    grad_w_value = inner_left(normed, values_grad)
    grad_b_value = column_sum(values_grad)
    normed_grad = (
        outer_right(query_grad, w_query)
        + outer_right(keys_grad, w_key)
        + outer_right(values_grad, w_value)
    )
    normed_grad = place_columns(normed_grad, outer_right(logit_one_all, gate1_w), start_col)
    normed_share = lax.psum_scatter(
        normed_grad.astype(jnp.bfloat16), "tensor", scatter_dimension=0, tiled=True
    ).astype(jnp.float32)
    input_back, grad_norm1_gain, grad_norm1_bias = norm_backward(
        normed_share, unit_one, inverse_one, norm1_gain.astype(jnp.float32)
    )
    input_grad = middle_grad + input_back
    norm_sums = lax.psum(
        (
            grad_norm1_gain,
            grad_norm1_bias,
            grad_norm2_gain,
            grad_norm2_bias,
            grad_b_out,
            grad_gate1_b,
        ),
        ("dp", "tensor"),
    )
    attention_grads = (
        grad_w_query,
        grad_b_query,
        grad_w_key,
        grad_w_value,
        grad_b_value,
        grad_w_out,
        grad_gate1_w,
    )
    every_grad = lax.psum(
        (
            grad_w_query,
            grad_b_query,
            grad_w_key,
            grad_w_value,
            grad_b_value,
            grad_w_out,
            grad_gate1_w,
            grad_w_in,
            grad_b_in,
            grad_w_back,
            grad_b_back,
            grad_gate2_w,
            grad_gate2_b,
        ),
        "dp",
    )
    attention_grads = every_grad[0:7]
    ffn_grads = every_grad[7:13]
    return (
        result.astype(jnp.bfloat16),
        input_grad,
        norm_sums[0],
        norm_sums[1],
        attention_grads[0],
        attention_grads[1],
        attention_grads[2],
        attention_grads[3],
        attention_grads[4],
        attention_grads[5],
        norm_sums[4],
        attention_grads[6],
        norm_sums[5],
        norm_sums[2],
        norm_sums[3],
        ffn_grads[0],
        ffn_grads[1],
        ffn_grads[2],
        ffn_grads[3],
        ffn_grads[4],
        ffn_grads[5],
    )


def solution(mesh):
    placed = (
        P(("dp", "tensor"), None),
        P("dp", None),
        P(),
        P(),
        P(None, "tensor"),
        P("tensor"),
        P(None, "tensor"),
        P(None, "tensor"),
        P("tensor"),
        P("tensor", None),
        P(),
        P("tensor", None),
        P(),
        P(),
        P(),
        P(None, "tensor"),
        P("tensor"),
        P("tensor", None),
        P(),
        P("tensor", None),
        P(),
        P(("dp", "tensor"), None),
    )
    return jax.shard_map(
        body,
        mesh=mesh,
        in_specs=placed,
        out_specs=(
            P(("dp", "tensor"), None),
            P(("dp", "tensor"), None),
            P(),
            P(),
            P(None, "tensor"),
            P("tensor"),
            P(None, "tensor"),
            P(None, "tensor"),
            P("tensor"),
            P("tensor", None),
            P(),
            P("tensor", None),
            P(),
            P(),
            P(),
            P(None, "tensor"),
            P("tensor"),
            P("tensor", None),
            P(),
            P("tensor", None),
            P(),
        ),
        check_vma=False,
    )
```

profile of v0, /device:TPU:0, one launch (start us, length us, event | category | flops | bytes accessed | tf_op | source)
XLA Modules:
  0.0 718.7 jit_solution(1008536278620861501)
XLA Ops:
  16.1 1.9 fusion.52
  18.0 14.4 %all-gather.13.cloned.1.call-done = bf16[1024,512]{1,0:T(8,128)(2,1)} async-done(((bf16[256,512]{1,0:T(8,128)(2,1)}), bf16[1024,512]{1,0:T(8,128)(2,1)}) %all-gather.13.cloned.1.call-update) | async-done | bytes 1048592 | tf_op jit(solution)/shard_map/all_gather | solution.py:186
  36.2 8.7 %while.38 = (s32[]{:T(128)}, bf16[2,2,512,64]{2,3,1,0:T(8,128)(2,1)}, f32[2,2,512,1]{2,1,3,0:T(2,128)S(1)}, pred[2,512,1024]{2,1,0:T(8,128)(4,1)S(1)}, bf16[2,2,...) while((s32[]{:T(128)}, ...), condition=%wide.region_18.19_spmd, body=%wide.region_15.18_spmd.sunk | while | flops 279977984 | bytes 18268324 | solution.py:101
  48.9 2.7 fusion.116
  54.8 25.5 %reduce-scatter.21.cloned.1.call-done = f32[256,512]{1,0:T(8,128)} async-done(((f32[1024,512]{1,0:T(8,128)}), f32[256,512]{1,0:T(8,128)}) %reduce-scatter.21.cloned.1.call-update) | async-done | bytes 524304 | tf_op jit(solution)/shard_map/reduce_scatter | solution.py:194
  80.3 34.1 %reduce-scatter.19.cloned.1.call-done = f32[256,512]{1,0:T(8,128)} async-done(((f32[1024,512]{1,0:T(8,128)}), f32[256,512]{1,0:T(8,128)}) %reduce-scatter.19.cloned.1.call-update) | async-done | bytes 524304 | tf_op jit(solution)/shard_map/reduce_scatter | solution.py:195
  118.3 16.8 %all-gather.15.cloned.1.call-done = bf16[1024,512]{1,0:T(8,128)(2,1)} async-done(((bf16[256,512]{1,0:T(8,128)(2,1)}), bf16[1024,512]{1,0:T(8,128)(2,1)}) %all-gather.15.cloned.1.call-update) | async-done | bytes 1048592 | tf_op jit(solution)/shard_map/all_gather | solution.py:203
  135.1 2.7 fusion.112
  138.6 30.8 %reduce-scatter.23.cloned.1.call-done = f32[256,512]{1,0:T(8,128)} async-done(((f32[1024,512]{1,0:T(8,128)}), f32[256,512]{1,0:T(8,128)}) %reduce-scatter.23.cloned.1.call-update) | async-done | bytes 524304 | tf_op jit(solution)/shard_map/reduce_scatter | solution.py:209
  169.5 2.0 fusion.100
  172.8 3.4 fusion.134
  176.2 12.2 %all-gather.17.cloned.1.call-done = bf16[1024,512]{1,0:T(8,128)(2,1)} async-done(((bf16[256,512]{1,0:T(8,128)(2,1)}), bf16[1024,512]{1,0:T(8,128)(2,1)}) %all-gather.17.cloned.1.call-update) | async-done | bytes 1048592 | tf_op jit(solution)/shard_map/all_gather | solution.py:312
  188.4 5.5 convert_reduce_fusion.2
  194.8 2.0 fusion.136
  198.2 30.3 %reduce-scatter.25.cloned.1.call-done = f32[256,512]{1,0:T(8,128)} async-done(((f32[1024,512]{1,0:T(8,128)}), f32[256,512]{1,0:T(8,128)}) %reduce-scatter.25.cloned.1.call-update) | async-done | bytes 524304 | tf_op jit(solution)/shard_map/reduce_scatter | solution.py:208
  228.5 2.2 fusion.102
  230.9 3.4 fusion.135
  234.4 13.2 %all-gather.19.cloned.1.call-done = bf16[1024,512]{1,0:T(8,128)(2,1)} async-done(((bf16[256,512]{1,0:T(8,128)(2,1)}), bf16[1024,512]{1,0:T(8,128)(2,1)}) %all-gather.19.cloned.1.call-update) | async-done | bytes 1048592 | tf_op jit(solution)/shard_map/all_gather | solution.py:313
  247.6 2.7 fusion.69
  251.1 30.8 %reduce-scatter.27.cloned.1.call-done = f32[256,512]{1,0:T(8,128)} async-done(((f32[1024,512]{1,0:T(8,128)}), f32[256,512]{1,0:T(8,128)}) %reduce-scatter.27.cloned.1.call-update) | async-done | bytes 524304 | tf_op jit(solution)/shard_map/reduce_scatter | solution.py:327
  281.9 2.1 multiply_reduce_fusion.1
  284.1 3.3 convert_reduce_fusion.6
  289.6 16.1 %all-gather.21.cloned.1.call-done = bf16[1024,512]{1,0:T(8,128)(2,1)} async-done(((bf16[256,512]{1,0:T(8,128)(2,1)}), bf16[1024,512]{1,0:T(8,128)(2,1)}) %all-gather.21.cloned.1.call-update) | async-done | bytes 1048592 | tf_op jit(solution)/shard_map/all_gather | solution.py:338
  305.7 2.4 convolution_convert_fusion
  311.7 16.5 %while.39 = (s32[]{:T(128)}, f32[2,1024,64]{1,2,0:T(8,128)}, f32[2,1024,64]{1,2,0:T(8,128)}, bf16[2,2,512,64]{2,3,1,0:T(8,128)(2,1)}, pred[2,512,1024]{2,1,0:T(8...) while((s32[]{:T(128)}, f32[2,1024,64]{1,2,0:T(8,128)}, ...), condition=%wide.region_29.30_spmd.clone, body=%wide.region_27.29_spmd.clone.sunk | while | flops 687602688 | bytes 50229632 | solution.py:148
  334.2 2.7 fusion.68
  336.9 2.7 convert_element_type.273
  343.1 21.6 %reduce-scatter.29.cloned.1.call-done = bf16[256,512]{1,0:T(8,128)(2,1)} async-done(((bf16[1024,512]{1,0:T(8,128)(2,1)}), bf16[256,512]{1,0:T(8,128)(2,1)}) %reduce-scatter.29.cloned.1.call-update) | async-done | bytes 262160 | tf_op jit(solution)/shard_map/reduce_scatter | solution.py:359
  364.7 1.9 fusion.105
  366.6 2.4 fusion.93
  370.4 15.5 %all-gather.9.cloned.1.call-done = bf16[1024,512]{1,0:T(8,128)(2,1)} async-done(((bf16[256,512]{1,0:T(8,128)(2,1)}), bf16[1024,512]{1,0:T(8,128)(2,1)}) %all-gather.9.cloned.1.call-update) | async-done | bytes 1048592 | tf_op jit(solution)/shard_map/all_gather | solution.py:186
  385.9 2.4 fusion.71
  391.9 2.7 fusion.108
  394.9 2.4 convolution_convert_fusion.2
  397.3 2.4 fusion.72
  400.4 10.8 %while.37 = (s32[]{:T(128)}, bf16[2,2,512,64]{2,3,1,0:T(8,128)(2,1)}, pred[2,512,1024]{2,1,0:T(8,128)(4,1)S(1)}, bf16[2,2,512,64]{2,3,1,0:T(8,128)(2,1)}, bf16[2...) while((s32[]{:T(128)}, bf16[2,2,512,64]{2,3,1,0:T(8,128)(2,1)}, ...), condition=%wide.region_6.7_spmd, body=%wide.region_3.0_spmd.sunk | while | flops 279973888 | bytes 19304628 | solution.py:101
  400.5 2.1 fusion.236
  405.9 2.1 fusion.236
  414.5 11.7 %reduce-scatter.11.cloned.1.call-done = f32[256,512]{1,0:T(8,128)} async-done(((f32[1024,512]{1,0:T(8,128)}), f32[256,512]{1,0:T(8,128)}) %reduce-scatter.11.cloned.1.call-update) | async-done | bytes 524304 | tf_op jit(solution)/shard_map/reduce_scatter | solution.py:195
  426.2 34.0 %reduce-scatter.13.cloned.1.call-done = f32[256,512]{1,0:T(8,128)} async-done(((f32[1024,512]{1,0:T(8,128)}), f32[256,512]{1,0:T(8,128)}) %reduce-scatter.13.cloned.1.call-update) | async-done | bytes 524304 | tf_op jit(solution)/shard_map/reduce_scatter | solution.py:194
  462.9 16.8 %all-gather.11.cloned.1.call-done = bf16[1024,512]{1,0:T(8,128)(2,1)} async-done(((bf16[256,512]{1,0:T(8,128)(2,1)}), bf16[1024,512]{1,0:T(8,128)(2,1)}) %all-gather.11.cloned.1.call-update) | async-done | bytes 1048592 | tf_op jit(solution)/shard_map/all_gather | solution.py:203
  479.7 4.1 fusion.70
  484.7 2.7 fusion.106
  487.4 3.4 fusion.144
  501.2 22.1 %all-reduce.1 = (f32[128]{0:T(128)}, f32[128]{0:T(128)}, f32[512]{0:T(512)}, f32[512]{0:T(512)}, f32[512]{0:T(512)}) all-reduce(f32[128]{0:T(128)S(1)} %reduce_sum.253, f32[128]{0:T(128)S(1)} %reduce_sum.255, f32[512]{0:T(512)S(1)} %copy-done.71, f32[512]{0:T(512)S(1)} %convert_reduce_fusion.1, ...), channel_id=1, replica_groups=mesh['dp'=8,'tensor'=4] {'dp'}, use_global_device_ids=true, to_apply=%region_39.40 | all-reduce | flops 1792 | bytes 14336 | tf_op jit(solution)/shard_map/psum | solution.py:386
  523.4 37.1 %all-reduce = (f32[512]{0:T(512)}, f32[512]{0:T(512)}, f32[512]{0:T(512)}, f32[512]{0:T(512)}, f32[512]{0:T(512)}, /*index=5*/f32[512]{0:T(512)}) all-reduce(f32[512]{0:T(512)S(1)} %copy-done.62, f32[512]{0:T(512)S(1)} %copy-done.63, f32[512]{0:T(512)S(1)} %copy-done.61, ...), channel_id=1, replica_groups=mesh['dp'=8,'tensor'=4] {'dp','tensor'}, use_global_device_ids=true, to_apply=%region_34.35 | all-reduce | flops 3072 | bytes 24576 | tf_op jit(solution)/shard_map/psum | solution.py:366
  560.4 2.2 add_convert_fusion.1
  562.6 139.3 %all-reduce.5.cloned.1.call-done = (f32[512,128]{1,0:T(8,128)}, f32[512,128]{1,0:T(8,128)}, f32[512,128]{1,0:T(8,128)}, f32[128,512]{1,0:T(8,128)}, f32[128,512]...) async-done(((f32[512,128]{1,0:T(8,128)}, f32[512,128]{1,0:T(8,128)}, f32[512,128]{1,0:T(8,128)}, f32[128,512]{1,0:T(8,128)}, ...) | async-done | bytes 3670032 | tf_op jit(solution)/shard_map/psum | solution.py:386
  (350 shorter events, 108.4 us)
Async XLA Ops:
  7.2 181.2 %copy-start = (bf16[512,512]{1,0:T(8,128)(2,1)S(1)}, bf16[512,512]{1,0:T(8,128)(2,1)}, u32[]{:S(2)}) copy-start(bf16[512,512]{1,0:T(8,128)(2,1)} %param.45) | copy-start | bytes 1572868
  7.2 25.2 %copy-start.23 = (bf16[512,128]{1,0:T(8,128)(2,1)S(1)}, bf16[512,128]{1,0:T(8,128)(2,1)}, u32[]{:S(2)}) copy-start(bf16[512,128]{1,0:T(8,128)(2,1)} %param.32) | copy-start | bytes 393220
  7.2 25.2 %all-gather.13.cloned.1.call-start = ((), (), s32[]{:S(2)}) async-start(), calls=%async_computation.16 | async-start | bytes 1310720 | tf_op jit(solution)/shard_map/all_gather | solution.py:186
  8.4 25.8 %copy-start.48 = (f32[256]{0:T(256)}, f32[256]{0:T(256)S(1)}, u32[]{:S(2)}) copy-start(f32[256]{0:T(256)S(1)} %broadcast_multiply_fusion.5) | copy-start | bytes 3076
  9.6 24.7 %copy-start.52 = (f32[256]{0:T(256)}, f32[256]{0:T(256)S(1)}, u32[]{:S(2)}) copy-start(f32[256]{0:T(256)S(1)} %add_rsqrt_fusion.1) | copy-start | bytes 3076
  11.0 23.5 %copy-start.25 = (bf16[512,128]{1,0:T(8,128)(2,1)S(1)}, bf16[512,128]{1,0:T(8,128)(2,1)}, u32[]{:S(2)}) copy-start(bf16[512,128]{1,0:T(8,128)(2,1)} %param.34) | copy-start | bytes 393220
  12.9 67.5 %reduce-scatter.21.cloned.1.call-start = ((), (), s32[]{:S(2)}) async-start(), calls=%async_computation.18 | async-start | bytes 2621440 | tf_op jit(solution)/shard_map/reduce_scatter | solution.py:194
  18.0 17.0 %copy-start.27 = (bf16[512,128]{1,0:T(8,128)(2,1)S(1)}, bf16[512,128]{1,0:T(8,128)(2,1)}, u32[]{:S(2)}) copy-start(bf16[512,128]{1,0:T(8,128)(2,1)} %param.35) | copy-start | bytes 393220
  36.2 10.7 %copy-start.22 = (bf16[128,512]{1,0:T(8,128)(2,1)S(1)}, bf16[128,512]{1,0:T(8,128)(2,1)}, u32[]{:S(2)}) copy-start(bf16[128,512]{1,0:T(8,128)(2,1)} %param.37) | copy-start | bytes 393220
  44.9 3.9 copy-start.6
  48.8 65.7 %reduce-scatter.19.cloned.1.call-start = ((), (), s32[]{:S(2)}) async-start(), calls=%async_computation.17 | async-start | bytes 2621440 | tf_op jit(solution)/shard_map/reduce_scatter | solution.py:195
  48.8 65.6 %copy-start.2 = (bf16[256,512]{1,0:T(8,128)(2,1)S(1)}, bf16[256,512]{1,0:T(8,128)(2,1)}, u32[]{:S(2)}) copy-start(bf16[256,512]{1,0:T(8,128)(2,1)} %param.28) | copy-start | bytes 786436
  51.6 83.6 %all-gather.15.cloned.1.call-start = ((), (), s32[]{:S(2)}) async-start(), calls=%async_computation.19 | async-start | bytes 1310720 | tf_op jit(solution)/shard_map/all_gather | solution.py:203
  52.3 63.7 %copy-start.51 = (f32[512]{0:T(512)}, f32[512]{0:T(512)S(1)}, u32[]{:S(2)}) copy-start(f32[512]{0:T(512)S(1)} %convert_element_type.253) | copy-start | bytes 6148
  116.0 21.9 %copy-start.50 = (f32[256]{0:T(256)}, f32[256]{0:T(256)S(1)}, u32[]{:S(2)}) copy-start(f32[256]{0:T(256)S(1)} %broadcast_multiply_fusion.4) | copy-start | bytes 3076
  118.2 51.2 %reduce-scatter.23.cloned.1.call-start = ((), (), s32[]{:S(2)}) async-start(), calls=%async_computation.20 | async-start | bytes 2621440 | tf_op jit(solution)/shard_map/reduce_scatter | solution.py:209
  137.9 50.5 %all-gather.17.cloned.1.call-start = ((), (), s32[]{:S(2)}) async-start(), calls=%async_computation.21 | async-start | bytes 1310720 | tf_op jit(solution)/shard_map/all_gather | solution.py:312
  171.5 57.0 %reduce-scatter.25.cloned.1.call-start = ((), (), s32[]{:S(2)}) async-start(), calls=%async_computation.22 | async-start | bytes 2621440 | tf_op jit(solution)/shard_map/reduce_scatter | solution.py:208
  196.9 50.7 %all-gather.19.cloned.1.call-start = ((), (), s32[]{:S(2)}) async-start(), calls=%async_computation.23 | async-start | bytes 1310720 | tf_op jit(solution)/shard_map/all_gather | solution.py:313
  230.7 51.2 %reduce-scatter.27.cloned.1.call-start = ((), (), s32[]{:S(2)}) async-start(), calls=%async_computation.24 | async-start | bytes 2621440 | tf_op jit(solution)/shard_map/reduce_scatter | solution.py:327
  250.3 55.4 %all-gather.21.cloned.1.call-start = ((), (), s32[]{:S(2)}) async-start(), calls=%async_computation.25 | async-start | bytes 1310720 | tf_op jit(solution)/shard_map/all_gather | solution.py:338
  281.9 5.5 copy-start.11
  288.8 45.3 %all-gather.23.cloned.1.call-start = ((), (), s32[]{:S(2)}) async-start(), calls=%async_computation.26 | async-start | bytes 1310720 | tf_op jit(solution)/shard_map/all_gather | solution.py:339
  289.6 75.1 %reduce-scatter.29.cloned.1.call-start = ((), (), s32[]{:S(2)}) async-start(), calls=%async_computation.27 | async-start | bytes 1310720 | tf_op jit(solution)/shard_map/reduce_scatter | solution.py:359
  336.9 27.8 %copy-start.49 = (f32[256]{0:T(256)S(1)}, f32[256]{0:T(256)}, u32[]{:S(2)}) copy-start(f32[256]{0:T(256)} %copy-done.48) | copy-start | bytes 3076
  336.9 27.8 %copy-start.53 = (f32[256]{0:T(256)S(1)}, f32[256]{0:T(256)}, u32[]{:S(2)}) copy-start(f32[256]{0:T(256)} %copy-done.52) | copy-start | bytes 3076
  339.6 46.3 %all-gather.9.cloned.1.call-start = ((), (), s32[]{:S(2)}) async-start(), calls=%async_computation.10 | async-start | bytes 1310720 | tf_op jit(solution)/shard_map/all_gather | solution.py:186
  369.0 57.2 %reduce-scatter.11.cloned.1.call-start = ((), (), s32[]{:S(2)}) async-start(), calls=%async_computation.11 | async-start | bytes 2621440 | tf_op jit(solution)/shard_map/reduce_scatter | solution.py:195
  394.6 65.6 %reduce-scatter.13.cloned.1.call-start = ((), (), s32[]{:S(2)}) async-start(), calls=%async_computation.12 | async-start | bytes 2621440 | tf_op jit(solution)/shard_map/reduce_scatter | solution.py:194
  414.4 48.5 %copy-start.68 = (bf16[512]{0:T(512)(128)(2,1)S(1)}, bf16[512]{0:T(512)(128)(2,1)}, u32[]{:S(2)}) copy-start(bf16[512]{0:T(512)(128)(2,1)} %param.44) | copy-start | bytes 3076
  414.4 65.3 %copy-start.21 = (bf16[512,512]{1,0:T(8,128)(2,1)S(1)}, bf16[512,512]{1,0:T(8,128)(2,1)}, u32[]{:S(2)}) copy-start(bf16[512,512]{1,0:T(8,128)(2,1)} %param.43) | copy-start | bytes 1572868
  414.4 65.3 %all-gather.11.cloned.1.call-start = ((), (), s32[]{:S(2)}) async-start(), calls=%async_computation.13 | async-start | bytes 1310720 | tf_op jit(solution)/shard_map/all_gather | solution.py:203
  461.7 22.1 %copy-start.9 = (f32[256,512]{1,0:T(8,128)}, f32[256,512]{1,0:T(8,128)S(1)}, u32[]{:S(2)}) copy-start(f32[256,512]{1,0:T(8,128)S(1)} %get-tuple-element.332) | copy-start | bytes 1572868
  462.8 97.6 %reduce-scatter.17.cloned.1.call-start = ((), (), s32[]{:S(2)}) async-start(), calls=%async_computation.15 | async-start | bytes 2621440 | tf_op jit(solution)/shard_map/reduce_scatter | solution.py:208
  483.8 76.7 %reduce-scatter.15.cloned.1.call-start = ((), (), s32[]{:S(2)}) async-start(), calls=%async_computation.14 | async-start | bytes 2621440 | tf_op jit(solution)/shard_map/reduce_scatter | solution.py:209
  487.4 214.6 %all-reduce.5.cloned.1.call-start = ((), (), s32[]{:S(2)}) async-start(), calls=%async_computation.28 | async-start | bytes 7340032 | tf_op jit(solution)/shard_map/psum | solution.py:386
  487.4 3.4 copy-start.16
  487.4 3.4 copy-start.30
  499.9 23.4 %copy-start.58 = (f32[512]{0:T(512)S(1)}, f32[512]{0:T(512)}, u32[]{:S(2)}) copy-start(f32[512]{0:T(512)} %get-tuple-element.247) | copy-start | bytes 6148
  499.9 23.4 %copy-start.59 = (f32[512]{0:T(512)S(1)}, f32[512]{0:T(512)}, u32[]{:S(2)}) copy-start(f32[512]{0:T(512)} %get-tuple-element.252) | copy-start | bytes 6148
  499.9 23.4 %copy-start.60 = (f32[512]{0:T(512)S(1)}, f32[512]{0:T(512)}, u32[]{:S(2)}) copy-start(f32[512]{0:T(512)} %get-tuple-element.324) | copy-start | bytes 6148
  499.9 23.4 %copy-start.61 = (f32[512]{0:T(512)S(1)}, f32[512]{0:T(512)}, u32[]{:S(2)}) copy-start(f32[512]{0:T(512)} %get-tuple-element.327) | copy-start | bytes 6148
  499.9 23.4 %copy-start.62 = (f32[512]{0:T(512)S(1)}, f32[512]{0:T(512)}, u32[]{:S(2)}) copy-start(f32[512]{0:T(512)} %get-tuple-element.250) | copy-start | bytes 6148
  499.9 23.4 %copy-start.63 = (f32[512]{0:T(512)S(1)}, f32[512]{0:T(512)}, u32[]{:S(2)}) copy-start(f32[512]{0:T(512)} %get-tuple-element.254) | copy-start | bytes 6148
  499.9 60.5 %copy-start.10 = (f32[256,512]{1,0:T(8,128)S(1)}, f32[256,512]{1,0:T(8,128)}, u32[]{:S(2)}) copy-start(f32[256,512]{1,0:T(8,128)} %copy-done.9) | copy-start | bytes 1572868
  701.9 6.9 copy-start.46
  701.9 7.6 %copy-start.34 = (f32[512,512]{1,0:T(8,128)S(1)}, f32[512,512]{1,0:T(8,128)}, u32[]{:S(2)}) copy-start(f32[512,512]{1,0:T(8,128)} %get-tuple-element.593) | copy-start | bytes 3145732
  703.7 6.8 copy-start.33
  (57 other events, 81.4 us)
Sparse Core Ops, SparseCore 0:
  13.0 19.4 all-gather.12
  48.9 31.4 reduce-scatter.20
  83.0 31.3 reduce-scatter.18
  118.4 16.7 all-gather.14
  138.0 31.4 reduce-scatter.22
  171.6 16.7 all-gather.16
  197.0 31.4 reduce-scatter.24
  230.8 16.7 all-gather.18
  250.5 31.4 reduce-scatter.26
  289.0 16.7 all-gather.20
  307.9 16.7 all-gather.22
  339.7 24.8 reduce-scatter.28
  369.1 16.7 all-gather.8
  394.7 31.4 reduce-scatter.10
  428.7 31.4 reduce-scatter.12
  462.9 16.7 all-gather.10
  483.9 31.4 reduce-scatter.16
  517.9 31.5 reduce-scatter.14
  555.9 145.9 all-reduce.4
where the time goes:
time: 720 us; the launch traced here: 719 us
  waiting for transfers between devices  464 us (64%)
  matrix products  87.1 us (12%)
  blocking collectives  59.2 us (8%)
  other arithmetic  56.5 us (8%)
  local copies, waits for them, and re-layouts  35.3 us (5%)
  between operations  14.7 us (2%)
    psum x1, waiting for transfers between devices, body(): lax.psum((grad_w_query, grad_b_query, grad_w_key, grad_w_value, grad_b_va...  139 us
    reduce_scatter x2, waiting for transfers between devices, forward_pass(): lax.psum_scatter(matmul(attended, w_out), 'tensor', scatter_dimension=0,...  59.5 us
    reduce_scatter x2, waiting for transfers between devices, forward_pass(): lax.psum_scatter(matmul(gate_rows, gate1_w), 'tensor', scatter_dimension=...  45.8 us
    psum x1, blocking collectives, body(): lax.psum((grad_norm1_gain, grad_norm1_bias, grad_norm2_gain, grad_norm2_b...  37.1 us
    dot_general x15, matrix products, matmul(): return jnp.dot(left, right, preferred_element_type=jnp.float32)  33.9 us
    all_gather x2, waiting for transfers between devices, forward_pass(): lax.all_gather(normed_two_part.astype(jnp.bfloat16), 'tensor', axis=0, ti...  33.6 us
    reduce_scatter x1, waiting for transfers between devices, body(): lax.psum_scatter(normed_two_grad, 'tensor', scatter_dimension=0, tiled=True)  30.8 us
    reduce_scatter x2, waiting for transfers between devices, forward_pass(): lax.psum_scatter(matmul(gate_rows_two, gate2_w), 'tensor', scatter_dimens...  30.8 us
  transfers between devices with their start and end apart: 19, of which 16 were waited for; matrix products, arithmetic and copies ran while one was open for 12% of the time, Pallas kernels for 0%

commit v1 on v0

--- a/solution.py
+++ b/solution.py
@@ -5,6 +5,27 @@
 
 HD = 64
 EPSILON = 1e-05
+
+
+def ring_gather(x, axis, dim):
+    size, position, extent = (lax.axis_size(axis), lax.axis_index(axis), x.shape[dim])
+    upward = [(i, (i + 1) % size) for i in range(size)]
+    behind = [(i, (i - 1) % size) for i in range(size)]
+    result = jnp.zeros((*x.shape[:dim], size * extent, *x.shape[dim + 1 :]), x.dtype)
+    result = lax.dynamic_update_slice_in_dim(result, x, position * extent, axis=dim)
+    from_left = from_right = x
+    middle = size // 2
+    for step in range(1, middle + 1):
+        from_left = lax.ppermute(from_left, axis, upward)
+        result = lax.dynamic_update_slice_in_dim(
+            result, from_left, (position - step) % size * extent, axis=dim
+        )
+        if step < size - middle:
+            from_right = lax.ppermute(from_right, axis, behind)
+            result = lax.dynamic_update_slice_in_dim(
+                result, from_right, (position + step) % size * extent, axis=dim
+            )
+    return result
 
 
 def matmul(left, right):
@@ -183,7 +204,7 @@
         inputs, norm1_gain.astype(jnp.float32), norm1_bias.astype(jnp.float32)
     )
     normed_low = normed_part.astype(jnp.bfloat16)
-    normed = lax.all_gather(normed_low, "tensor", axis=0, tiled=True)
+    normed = ring_gather(normed_low, "tensor", 0)
     query = (matmul(normed, w_query) + b_query.astype(jnp.float32)).astype(jnp.bfloat16)
     keys = matmul(normed, w_key).astype(jnp.bfloat16)
     values = (matmul(normed, w_value) + b_value.astype(jnp.float32)).astype(jnp.bfloat16)

time: 720 us -> 687 us (0.954)
  waiting for transfers between devices: 464 us -> 413 us
  local copies, waits for them, and re-layouts: 35.3 us -> 42.8 us
    all_gather x2 -> x0, waiting for transfers between devices: 29.9 us -> none  [forward_pass(): normed = lax.all_gather(normed_low, 'tensor', axis=0, tiled=True)]
    reduce_scatter x1, waiting for transfers between devices: 21.6 us -> 0.01 us  [body(): lax.psum_scatter(normed_grad.astype(jnp.bfloat16), 'tensor', scatter_dime...]
    ppermute x0 -> x6, waiting for transfers between devices: none -> 15.4 us  [the longest x4 15.4 us: ring_gather(): from_left = lax.ppermute(from_left, axis, upward)]
    all_gather x1, waiting for transfers between devices: 13.2 us -> 0.01 us  [body(): lax.all_gather(logit_two_grad, 'tensor', axis=0, tiled=True)]
    all_gather x2, waiting for transfers between devices: 33.6 us -> 21.1 us  [forward_pass(): lax.all_gather(normed_two_part.astype(jnp.bfloat16), 'tensor', axis=0, ti...]
    reduce_scatter x2, waiting for transfers between devices: 45.8 us -> 34.8 us  [forward_pass(): lax.psum_scatter(matmul(gate_rows, gate1_w), 'tensor', scatter_dimension=...]
    psum x1, waiting for transfers between devices: 139 us -> 150 us  [body(): lax.psum((grad_w_query, grad_b_query, grad_w_key, grad_w_value, grad_b_va...]
    reduce_scatter x2, waiting for transfers between devices: 30.8 us -> 41.5 us  [forward_pass(): lax.psum_scatter(matmul(gate_rows_two, gate2_w), 'tensor', scatter_dimens...]
  transfers between devices with their start and end apart: 19 -> 23, of which waited for: 16 -> 17; matrix products, arithmetic and copies ran while one was open for 12% -> 18% of each run, Pallas kernels for 0% -> 0%
where the time goes in v1:
time: 687 us; the launch traced here: 685 us
  waiting for transfers between devices  413 us (60%)
  matrix products  86 us (13%)
  other arithmetic  60.6 us (9%)
  blocking collectives  59.6 us (9%)
  local copies, waits for them, and re-layouts  42.8 us (6%)
  between operations  14.8 us (2%)
  starting transfers between devices  8.21 us (1%)
    psum x1, waiting for transfers between devices, body(): lax.psum((grad_w_query, grad_b_query, grad_w_key, grad_w_value, grad_b_va...  150 us
    reduce_scatter x2, waiting for transfers between devices, forward_pass(): lax.psum_scatter(matmul(attended, w_out), 'tensor', scatter_dimension=0,...  63.6 us
    reduce_scatter x2, waiting for transfers between devices, forward_pass(): lax.psum_scatter(matmul(gate_rows_two, gate2_w), 'tensor', scatter_dimens...  41.5 us
    psum x1, blocking collectives, body(): lax.psum((grad_norm1_gain, grad_norm1_bias, grad_norm2_gain, grad_norm2_b...  37.4 us
    reduce_scatter x2, waiting for transfers between devices, forward_pass(): lax.psum_scatter(matmul(gate_rows, gate1_w), 'tensor', scatter_dimension=...  34.8 us
    dot_general x15, matrix products, matmul(): return jnp.dot(left, right, preferred_element_type=jnp.float32)  32.7 us
    reduce_scatter x1, waiting for transfers between devices, body(): lax.psum_scatter(normed_two_grad, 'tensor', scatter_dimension=0, tiled=True)  30.8 us
    reduce_scatter x2, waiting for transfers between devices, forward_pass(): lax.psum_scatter(matmul(hidden, w_back), 'tensor', scatter_dimension=0, t...  26.7 us
  transfers between devices with their start and end apart: 23, of which 17 were waited for; matrix products, arithmetic and copies ran while one was open for 18% of the time, Pallas kernels for 0%

profile of v1, /device:TPU:0, one launch (start us, length us, event | category | flops | bytes accessed | tf_op | source)
XLA Modules:
  0.0 685.3 jit_solution(7844050310625490319)
XLA Ops:
  13.4 2.0 collective-permute-start.4
  16.5 3.2 collective-permute-done.3
  19.7 2.7 collective-permute-start.5
  29.0 8.7 %while.38 = (s32[]{:T(128)}, bf16[2,2,512,64]{2,3,1,0:T(8,128)(2,1)}, f32[2,2,512,1]{2,1,3,0:T(2,128)S(1)}, pred[2,512,1024]{2,1,0:T(8,128)(4,1)S(1)}, bf16[2,2,...) while((s32[]{:T(128)}, ...), condition=%wide.region_18.19_spmd, body=%wide.region_15.18_spmd.sunk | while | flops 279977984 | bytes 18268324 | solution.py:122
  41.7 2.7 fusion.116
  47.6 29.4 %reduce-scatter.21.cloned.1.call-done = f32[256,512]{1,0:T(8,128)} async-done(((f32[1024,512]{1,0:T(8,128)}), f32[256,512]{1,0:T(8,128)}) %reduce-scatter.21.cloned.1.call-update) | async-done | bytes 524304 | tf_op jit(solution)/shard_map/reduce_scatter | solution.py:215
  77.1 34.1 %reduce-scatter.19.cloned.1.call-done = f32[256,512]{1,0:T(8,128)} async-done(((f32[1024,512]{1,0:T(8,128)}), f32[256,512]{1,0:T(8,128)}) %reduce-scatter.19.cloned.1.call-update) | async-done | bytes 524304 | tf_op jit(solution)/shard_map/reduce_scatter | solution.py:216
  115.0 16.8 %all-gather.9.cloned.1.call-done = bf16[1024,512]{1,0:T(8,128)(2,1)} async-done(((bf16[256,512]{1,0:T(8,128)(2,1)}), bf16[1024,512]{1,0:T(8,128)(2,1)}) %all-gather.9.cloned.1.call-update) | async-done | bytes 1048592 | tf_op jit(solution)/shard_map/all_gather | solution.py:224
  131.8 2.7 fusion.112
  135.3 30.8 %reduce-scatter.23.cloned.1.call-done = f32[256,512]{1,0:T(8,128)} async-done(((f32[1024,512]{1,0:T(8,128)}), f32[256,512]{1,0:T(8,128)}) %reduce-scatter.23.cloned.1.call-update) | async-done | bytes 524304 | tf_op jit(solution)/shard_map/reduce_scatter | solution.py:230
  166.2 2.0 fusion.100
  169.5 3.4 fusion.136
  172.9 12.2 %all-gather.11.cloned.1.call-done = bf16[1024,512]{1,0:T(8,128)(2,1)} async-done(((bf16[256,512]{1,0:T(8,128)(2,1)}), bf16[1024,512]{1,0:T(8,128)(2,1)}) %all-gather.11.cloned.1.call-update) | async-done | bytes 1048592 | tf_op jit(solution)/shard_map/all_gather | solution.py:333
  185.1 5.5 convert_reduce_fusion.2
  191.6 2.0 fusion.138
  198.6 26.7 %reduce-scatter.25.cloned.1.call-done = f32[256,512]{1,0:T(8,128)} async-done(((f32[1024,512]{1,0:T(8,128)}), f32[256,512]{1,0:T(8,128)}) %reduce-scatter.25.cloned.1.call-update) | async-done | bytes 524304 | tf_op jit(solution)/shard_map/reduce_scatter | solution.py:229
  225.3 2.2 fusion.102
  232.7 8.4 %collective-permute-done = bf16[256,512]{1,0:T(8,128)(2,1)} collective-permute-done((bf16[256,512]{1,0:T(8,128)(2,1)}, bf16[256,512]{1,0:T(8,128)(2,1)}, u32[]{:S(2)}, u32[]{:S(2)}) %collective-permute-start) | collective-permute-done | bytes 262176 | tf_op jit(solution)/shard_map/ppermute | solution.py:19
  246.2 2.0 collective-permute-done.2
  249.9 2.4 fusion.71
  252.3 1.9 reshape.261
  255.9 2.8 fusion.108
  258.7 2.4 convolution_convert_fusion.2
  261.1 2.5 fusion.72
  264.3 10.8 %while.37 = (s32[]{:T(128)}, bf16[2,2,512,64]{2,3,1,0:T(8,128)(2,1)}, pred[2,512,1024]{2,1,0:T(8,128)(4,1)S(1)}, bf16[2,2,512,64]{2,3,1,0:T(8,128)(2,1)}, bf16[2...) while((s32[]{:T(128)}, bf16[2,2,512,64]{2,3,1,0:T(8,128)(2,1)}, ...), condition=%wide.region_6.7_spmd, body=%wide.region_3.6_spmd.sunk | while | flops 279973888 | bytes 19304628 | solution.py:122
  264.4 2.1 fusion.238
  269.8 2.1 fusion.238
  278.3 3.4 fusion.137
  281.7 2.7 fusion.69
  290.2 34.2 %reduce-scatter.13.cloned.1.call-done = f32[256,512]{1,0:T(8,128)} async-done(((f32[1024,512]{1,0:T(8,128)}), f32[256,512]{1,0:T(8,128)}) %reduce-scatter.13.cloned.1.call-update) | async-done | bytes 524304 | tf_op jit(solution)/shard_map/reduce_scatter | solution.py:215
  327.4 30.8 %reduce-scatter.27.cloned.1.call-done = f32[256,512]{1,0:T(8,128)} async-done(((f32[1024,512]{1,0:T(8,128)}), f32[256,512]{1,0:T(8,128)}) %reduce-scatter.27.cloned.1.call-update) | async-done | bytes 524304 | tf_op jit(solution)/shard_map/reduce_scatter | solution.py:348
  358.2 2.1 multiply_reduce_fusion.1
  360.3 3.6 convert_reduce_fusion.6
  367.0 15.3 %all-gather.15.cloned.1.call-done = bf16[1024,512]{1,0:T(8,128)(2,1)} async-done(((bf16[256,512]{1,0:T(8,128)(2,1)}), bf16[1024,512]{1,0:T(8,128)(2,1)}) %all-gather.15.cloned.1.call-update) | async-done | bytes 1048592 | tf_op jit(solution)/shard_map/all_gather | solution.py:359
  382.3 2.4 convolution_convert_fusion
  388.2 16.5 %while.39 = (s32[]{:T(128)}, f32[2,1024,64]{1,2,0:T(8,128)}, f32[2,1024,64]{1,2,0:T(8,128)}, bf16[2,2,512,64]{2,3,1,0:T(8,128)(2,1)}, pred[2,512,1024]{2,1,0:T(8...) while((s32[]{:T(128)}, f32[2,1024,64]{1,2,0:T(8,128)}, ...), condition=%wide.region_29.30_spmd.clone, body=%wide.region_27.29_spmd.clone.sunk | while | flops 687602688 | bytes 50229632 | solution.py:169
  410.2 2.8 fusion.68
  413.0 2.8 convert_element_type.273
  415.9 4.2 all-gather.7.cloned.1.call-done
  420.1 4.1 fusion.70
  425.1 2.7 fusion.106
  428.1 3.4 fusion.146
  442.7 22.2 %all-reduce.1 = (f32[128]{0:T(128)}, f32[128]{0:T(128)}, f32[512]{0:T(512)}, f32[512]{0:T(512)}, f32[512]{0:T(512)}) all-reduce(f32[128]{0:T(128)S(1)} %reduce_sum.253, f32[128]{0:T(128)S(1)} %reduce_sum.255, f32[512]{0:T(512)S(1)} %copy-done.69, f32[512]{0:T(512)S(1)} %convert_reduce_fusion.1, ...), channel_id=1, replica_groups=mesh['dp'=8,'tensor'=4] {'dp'}, use_global_device_ids=true, to_apply=%region_39.40 | all-reduce | flops 1792 | bytes 14336 | tf_op jit(solution)/shard_map/psum | solution.py:407
  466.3 37.4 %all-reduce = (f32[512]{0:T(512)}, f32[512]{0:T(512)}, f32[512]{0:T(512)}, f32[512]{0:T(512)}, f32[512]{0:T(512)}, /*index=5*/f32[512]{0:T(512)}) all-reduce(f32[512]{0:T(512)S(1)} %get-tuple-element.250, f32[512]{0:T(512)S(1)} %get-tuple-element.254, f32[512]{0:T(512)S(1)} %copy-done.64, ...), channel_id=1, replica_groups=mesh['dp'=8,'tensor'=4] {'dp','tensor'}, use_global_device_ids=true, to_apply=%region_34.35 | all-reduce | flops 3072 | bytes 24576 | tf_op jit(solution)/shard_map/psum | solution.py:387
  503.7 2.0 fusion.93
  505.7 10.7 %reduce-scatter.15.cloned.1.call-done = f32[256,512]{1,0:T(8,128)} async-done(((f32[1024,512]{1,0:T(8,128)}), f32[256,512]{1,0:T(8,128)}) %reduce-scatter.15.cloned.1.call-update) | async-done | bytes 524304 | tf_op jit(solution)/shard_map/reduce_scatter | solution.py:230
  516.3 2.1 add_convert_fusion.1
  518.4 150.1 %all-reduce.5.cloned.1.call-done = (f32[512,128]{1,0:T(8,128)}, f32[512,128]{1,0:T(8,128)}, f32[512,128]{1,0:T(8,128)}, f32[128,512]{1,0:T(8,128)}, f32[128,512]...) async-done(((f32[512,128]{1,0:T(8,128)}, f32[512,128]{1,0:T(8,128)}, f32[512,128]{1,0:T(8,128)}, f32[128,512]{1,0:T(8,128)}, ...) | async-done | bytes 3670032 | tf_op jit(solution)/shard_map/psum | solution.py:407
  (362 shorter events, 126.1 us)
Async XLA Ops:
  7.2 177.9 %copy-start = (bf16[512,512]{1,0:T(8,128)(2,1)S(1)}, bf16[512,512]{1,0:T(8,128)(2,1)}, u32[]{:S(2)}) copy-start(bf16[512,512]{1,0:T(8,128)(2,1)} %param.45) | copy-start | bytes 1572868
  7.2 16.5 %copy-start.71 = (bf16[128]{0:T(256)(128)(2,1)S(1)}, bf16[128]{0:T(256)(128)(2,1)}, u32[]{:S(2)}) copy-start(bf16[128]{0:T(256)(128)(2,1)} %param.36) | copy-start | bytes 772
  7.2 16.5 %copy-start.70 = (bf16[128]{0:T(256)(128)(2,1)S(1)}, bf16[128]{0:T(256)(128)(2,1)}, u32[]{:S(2)}) copy-start(bf16[128]{0:T(256)(128)(2,1)} %param.33) | copy-start | bytes 772
  7.2 8.6 %copy-start.55 = (s32[1,1024]{1,0:T(1,128)S(1)}, s32[1,1024]{1,0:T(1,128)}, u32[]{:S(2)}) copy-start(s32[1,1024]{1,0:T(1,128)} %param.29) | copy-start | bytes 12292
  7.2 69.8 %reduce-scatter.21.cloned.1.call-start = ((), (), s32[]{:S(2)}) async-start(), calls=%async_computation.16 | async-start | bytes 2621440 | tf_op jit(solution)/shard_map/reduce_scatter | solution.py:215
  8.4 14.0 %copy-start.48 = (f32[256]{0:T(256)}, f32[256]{0:T(256)S(1)}, u32[]{:S(2)}) copy-start(f32[256]{0:T(256)S(1)} %broadcast_multiply_fusion.5) | copy-start | bytes 3076
  9.6 12.8 %copy-start.53 = (f32[256]{0:T(256)}, f32[256]{0:T(256)S(1)}, u32[]{:S(2)}) copy-start(f32[256]{0:T(256)S(1)} %add_rsqrt_fusion.1) | copy-start | bytes 3076
  11.0 15.6 %copy-start.23 = (bf16[512,128]{1,0:T(8,128)(2,1)S(1)}, bf16[512,128]{1,0:T(8,128)(2,1)}, u32[]{:S(2)}) copy-start(bf16[512,128]{1,0:T(8,128)(2,1)} %param.32) | copy-start | bytes 393220
  12.9 6.8 collective-permute-start.3
  13.4 10.4 %collective-permute-start.4 = (bf16[256,512]{1,0:T(8,128)(2,1)}, bf16[256,512]{1,0:T(8,128)(2,1)S(1)}, u32[]{:S(2)}, u32[]{:S(2)}) collective-permute-start(bf16[256,512]{1,0:T(8,128)(2,1)} %get-tuple-element.332), channel_id=1, source_target_pairs={{0,3},{1,0},{2,1},{3,2},{4,7},{5,4},{6,5},{7,6},{8,11},{9,8},{10,9... | collective-permute-start | bytes 786440 | tf_op jit(solution)/shard_map/ppermute | solution.py:24
  19.7 5.9 collective-permute-start.5
  29.0 10.7 %copy-start.22 = (bf16[128,512]{1,0:T(8,128)(2,1)S(1)}, bf16[128,512]{1,0:T(8,128)(2,1)}, u32[]{:S(2)}) copy-start(bf16[128,512]{1,0:T(8,128)(2,1)} %param.37) | copy-start | bytes 393220
  37.7 3.9 copy-start.5
  41.6 69.6 %reduce-scatter.19.cloned.1.call-start = ((), (), s32[]{:S(2)}) async-start(), calls=%async_computation.15 | async-start | bytes 2621440 | tf_op jit(solution)/shard_map/reduce_scatter | solution.py:216
  41.7 69.5 %copy-start.1 = (bf16[256,512]{1,0:T(8,128)(2,1)S(1)}, bf16[256,512]{1,0:T(8,128)(2,1)}, u32[]{:S(2)}) copy-start(bf16[256,512]{1,0:T(8,128)(2,1)} %param.28) | copy-start | bytes 786436
  44.4 87.5 %all-gather.9.cloned.1.call-start = ((), (), s32[]{:S(2)}) async-start(), calls=%async_computation.17 | async-start | bytes 1310720 | tf_op jit(solution)/shard_map/all_gather | solution.py:224
  45.1 67.6 %copy-start.51 = (f32[512]{0:T(512)}, f32[512]{0:T(512)S(1)}, u32[]{:S(2)}) copy-start(f32[512]{0:T(512)S(1)} %convert_element_type.253) | copy-start | bytes 6148
  112.7 21.9 %copy-start.50 = (f32[256]{0:T(256)}, f32[256]{0:T(256)S(1)}, u32[]{:S(2)}) copy-start(f32[256]{0:T(256)S(1)} %broadcast_multiply_fusion.4) | copy-start | bytes 3076
  114.9 51.2 %reduce-scatter.23.cloned.1.call-start = ((), (), s32[]{:S(2)}) async-start(), calls=%async_computation.18 | async-start | bytes 2621440 | tf_op jit(solution)/shard_map/reduce_scatter | solution.py:230
  134.6 50.5 %all-gather.11.cloned.1.call-start = ((), (), s32[]{:S(2)}) async-start(), calls=%async_computation.19 | async-start | bytes 1310720 | tf_op jit(solution)/shard_map/all_gather | solution.py:333
  135.3 37.5 %copy-start.52 = (f32[512]{0:T(512)}, f32[512]{0:T(512)S(1)}, u32[]{:S(2)}) copy-start(f32[512]{0:T(512)S(1)} %convert_element_type.257) | copy-start | bytes 6148
  168.2 57.1 %reduce-scatter.25.cloned.1.call-start = ((), (), s32[]{:S(2)}) async-start(), calls=%async_computation.20 | async-start | bytes 2621440 | tf_op jit(solution)/shard_map/reduce_scatter | solution.py:229
  193.7 88.0 %all-gather.13.cloned.1.call-start = ((), (), s32[]{:S(2)}) async-start(), calls=%async_computation.21 | async-start | bytes 1310720 | tf_op jit(solution)/shard_map/all_gather | solution.py:334
  227.5 62.8 %reduce-scatter.11.cloned.1.call-start = ((), (), s32[]{:S(2)}) async-start(), calls=%async_computation.10 | async-start | bytes 2621440 | tf_op jit(solution)/shard_map/reduce_scatter | solution.py:216
  230.9 10.2 %collective-permute-start = (bf16[256,512]{1,0:T(8,128)(2,1)}, bf16[256,512]{1,0:T(8,128)(2,1)}, u32[]{:S(2)}, u32[]{:S(2)}) collective-permute-start(bf16[256,512]{1,0:T(8,128)(2,1)} %get-tuple-element.336), channel_id=1, source_target_pairs={{0,1},{1,2},{2,3},{3,0},{4,5},{5,6},{6,7},{7,4},{8,9},{9,10},{10,1... | collective-permute-start | bytes 786440 | tf_op jit(solution)/shard_map/ppermute | solution.py:19
  230.9 13.6 %collective-permute-start.1 = (bf16[256,512]{1,0:T(8,128)(2,1)}, bf16[256,512]{1,0:T(8,128)(2,1)}, u32[]{:S(2)}, u32[]{:S(2)}) collective-permute-start(bf16[256,512]{1,0:T(8,128)(2,1)} %get-tuple-element.336), channel_id=1, source_target_pairs={{0,3},{1,0},{2,1},{3,2},{4,7},{5,4},{6,5},{7,6},{8,11},{9,8},{10,9... | collective-permute-start | bytes 786440 | tf_op jit(solution)/shard_map/ppermute | solution.py:24
  241.1 7.2 %collective-permute-start.2 = (bf16[256,512]{1,0:T(8,128)(2,1)}, bf16[256,512]{1,0:T(8,128)(2,1)}, u32[]{:S(2)}, u32[]{:S(2)}) collective-permute-start(bf16[256,512]{1,0:T(8,128)(2,1)} %collective-permute-done), channel_id=1, source_target_pairs={{0,1},{1,2},{2,3},{3,0},{4,5},{5,6},{6,7},{7,4},{8,9},{9,10},{10,1... | collective-permute-start | bytes 786440 | tf_op jit(solution)/shard_map/ppermute | solution.py:19
  258.7 65.7 %reduce-scatter.13.cloned.1.call-start = ((), (), s32[]{:S(2)}) async-start(), calls=%async_computation.11 | async-start | bytes 2621440 | tf_op jit(solution)/shard_map/reduce_scatter | solution.py:215
  278.2 80.0 %reduce-scatter.27.cloned.1.call-start = ((), (), s32[]{:S(2)}) async-start(), calls=%async_computation.22 | async-start | bytes 2621440 | tf_op jit(solution)/shard_map/reduce_scatter | solution.py:348
  284.5 97.9 %all-gather.15.cloned.1.call-start = ((), (), s32[]{:S(2)}) async-start(), calls=%async_computation.23 | async-start | bytes 1310720 | tf_op jit(solution)/shard_map/all_gather | solution.py:359
  365.4 44.8 %all-gather.17.cloned.1.call-start = ((), (), s32[]{:S(2)}) async-start(), calls=%async_computation.24 | async-start | bytes 1310720 | tf_op jit(solution)/shard_map/all_gather | solution.py:360
  366.0 54.1 %all-gather.7.cloned.1.call-start = ((), (), s32[]{:S(2)}) async-start(), calls=%async_computation.12 | async-start | bytes 1310720 | tf_op jit(solution)/shard_map/all_gather | solution.py:224
  366.8 98.2 %reduce-scatter.29.cloned.1.call-start = ((), (), s32[]{:S(2)}) async-start(), calls=%async_computation.25 | async-start | bytes 1310720 | tf_op jit(solution)/shard_map/reduce_scatter | solution.py:380
  413.0 7.1 %copy-start.21 = (bf16[512,512]{1,0:T(8,128)(2,1)S(1)}, bf16[512,512]{1,0:T(8,128)(2,1)}, u32[]{:S(2)}) copy-start(bf16[512,512]{1,0:T(8,128)(2,1)} %param.43) | copy-start | bytes 1572868
  415.8 89.9 %reduce-scatter.17.cloned.1.call-start = ((), (), s32[]{:S(2)}) async-start(), calls=%async_computation.14 | async-start | bytes 2621440 | tf_op jit(solution)/shard_map/reduce_scatter | solution.py:229
  424.2 92.1 %reduce-scatter.15.cloned.1.call-start = ((), (), s32[]{:S(2)}) async-start(), calls=%async_computation.13 | async-start | bytes 2621440 | tf_op jit(solution)/shard_map/reduce_scatter | solution.py:230
  427.8 240.7 %all-reduce.5.cloned.1.call-start = ((), (), s32[]{:S(2)}) async-start(), calls=%async_computation.26 | async-start | bytes 7340032 | tf_op jit(solution)/shard_map/psum | solution.py:407
  440.6 24.4 %copy-start.49 = (f32[256]{0:T(256)S(1)}, f32[256]{0:T(256)}, u32[]{:S(2)}) copy-start(f32[256]{0:T(256)} %copy-done.48) | copy-start | bytes 3076
  440.6 24.4 %copy-start.54 = (f32[256]{0:T(256)S(1)}, f32[256]{0:T(256)}, u32[]{:S(2)}) copy-start(f32[256]{0:T(256)} %copy-done.53) | copy-start | bytes 3076
  440.6 25.7 %copy-start.61 = (f32[512]{0:T(512)S(1)}, f32[512]{0:T(512)}, u32[]{:S(2)}) copy-start(f32[512]{0:T(512)} %get-tuple-element.247) | copy-start | bytes 6148
  440.6 25.7 %copy-start.62 = (f32[512]{0:T(512)S(1)}, f32[512]{0:T(512)}, u32[]{:S(2)}) copy-start(f32[512]{0:T(512)} %get-tuple-element.252) | copy-start | bytes 6148
  440.6 25.7 %copy-start.63 = (f32[512]{0:T(512)S(1)}, f32[512]{0:T(512)}, u32[]{:S(2)}) copy-start(f32[512]{0:T(512)} %get-tuple-element.324) | copy-start | bytes 6148
  440.6 25.7 %copy-start.64 = (f32[512]{0:T(512)S(1)}, f32[512]{0:T(512)}, u32[]{:S(2)}) copy-start(f32[512]{0:T(512)} %get-tuple-element.327) | copy-start | bytes 6148
  440.7 63.0 %copy-start.12 = (f32[256,512]{1,0:T(8,128)S(1)}, f32[256,512]{1,0:T(8,128)}, u32[]{:S(2)}) copy-start(f32[256,512]{1,0:T(8,128)} %copy-done.11) | copy-start | bytes 1572868
  440.7 75.6 %copy-start.9 = (f32[256,512]{1,0:T(8,128)S(1)}, f32[256,512]{1,0:T(8,128)}, u32[]{:S(2)}) copy-start(f32[256,512]{1,0:T(8,128)} %copy-done.8) | copy-start | bytes 1572868
  668.5 6.9 %copy-start.46 = (f32[128,512]{1,0:T(8,128)S(1)}, f32[128,512]{1,0:T(8,128)}, u32[]{:S(2)}) copy-start(f32[128,512]{1,0:T(8,128)} %get-tuple-element.592) | copy-start | bytes 786436
  668.5 7.6 %copy-start.34 = (f32[512,512]{1,0:T(8,128)S(1)}, f32[512,512]{1,0:T(8,128)}, u32[]{:S(2)}) copy-start(f32[512,512]{1,0:T(8,128)} %get-tuple-element.596) | copy-start | bytes 3145732
  670.3 6.8 copy-start.33
  (60 other events, 96.6 us)
Sparse Core Ops, SparseCore 0:
  41.7 35.3 reduce-scatter.20
  79.8 31.3 reduce-scatter.18
  115.1 16.7 all-gather.8
  134.7 31.4 reduce-scatter.22
  168.3 16.7 all-gather.10
  193.8 31.4 reduce-scatter.24
  227.6 19.7 all-gather.12
  258.8 31.4 reduce-scatter.10
  292.9 31.4 reduce-scatter.12
  326.8 31.4 reduce-scatter.26
  365.6 16.7 all-gather.14
  384.4 16.7 all-gather.16
  403.4 16.6 all-gather.6
  423.2 24.8 reduce-scatter.28
  450.5 32.1 reduce-scatter.16
  485.2 31.0 reduce-scatter.14
  522.6 145.9 all-reduce.4
